TPU v7x, 32 devices: a whole 2x2x4 slice. The times are simulated.
32 devices in a mesh: shot: 4 (over x, core), rcv: 8 (over z, y).
Axes of the slice: x: 2, y: 2, z: 4, core: 2. Of those that a mesh axis runs over, the one named last changes fastest.
Arguments:
- response: bfloat16 [128, 128, 64], P('shot', 'rcv'), may hold values from -0.0625 to 0.0625
- traces: bfloat16 [128, 64, 512], P('shot', 'rcv'), may hold values from -6 to 6
Outputs:
- multiples: bfloat16 [128, 64, 512], P('shot', 'rcv')
All inputs are finite; a program needn't handle non-finite values.
Results may differ from a plain program's by a relative error of at most 0.001.
Values may be sent and summed in bfloat16 or wider, within the bound.
A program may use at most 256 MiB of HBM per device.

v0:
```python
import jax
import jax.numpy as jnp
from jax import lax
from jax.sharding import PartitionSpec as P


def banded(resp_piece):
    shots_here = resp_piece.shape[0]
    rows_in = resp_piece.shape[1]
    tap_count = resp_piece.shape[2]
    reversed_taps = jnp.transpose(resp_piece[:, :, ::-1], (2, 0, 1))
    lead = jnp.zeros((1, shots_here, rows_in), resp_piece.dtype)
    trail = jnp.zeros((tap_count, shots_here, rows_in), resp_piece.dtype)
    pattern = jnp.concatenate([lead, reversed_taps, trail], axis=0)
    repeated = jnp.tile(pattern, (tap_count, 1, 1))[: 2 * tap_count * tap_count]
    return repeated.reshape(tap_count, 2 * tap_count, shots_here, rows_in)


def contract(resp_piece, data_piece):
    shots_here = resp_piece.shape[0]
    tap_count = resp_piece.shape[2]
    rows_in = data_piece.shape[0]
    rcv_here = data_piece.shape[1]
    samples = data_piece.shape[2]
    blocks = samples // tap_count
    band = banded(resp_piece)
    padded = jnp.pad(data_piece, ((0, 0), (0, 0), (tap_count, 0)))
    tiles = padded.reshape(rows_in, rcv_here, blocks + 1, tap_count)
    windows = jnp.concatenate([tiles[:, :, :blocks], tiles[:, :, 1:]], axis=3)
    product = jnp.einsum("uvsk,krbv->srbu", band, windows, preferred_element_type=jnp.float32)
    return product.reshape(shots_here, rcv_here * samples)


def shards(response, traces):
    shots_here = response.shape[0]
    rcv_here = traces.shape[1]
    samples = traces.shape[2]
    responses_all = lax.all_gather(response, "rcv", axis=1, tiled=True)
    running = contract(responses_all, lax.all_gather(traces, "shot", axis=0, tiled=True))
    return running.reshape(shots_here, rcv_here, samples).astype(jnp.bfloat16)


def solution(mesh):
    placed = (P("shot", "rcv", None), P("shot", "rcv", None))
    return jax.shard_map(
        shards, mesh=mesh, in_specs=placed, out_specs=P("shot", "rcv", None), check_vma=False
    )
```

profile of v0, /device:TPU:0, one launch (start us, length us, event | category | flops | bytes accessed | tf_op | source)
XLA Modules:
  0.0 322.5 jit_solution(11808536504618366029)
XLA Ops:
  6.5 0.0 all-gather.2.cloned.1.call-start
  6.5 0.7 all-gather.2.cloned.1.call-update
  7.3 34.9 %all_gather.7 = bf16[32,128,64]{2,1,0:T(8,128)(2,1)S(1)} all-gather(bf16[32,16,64]{2,1,0:T(8,128)(2,1)} %param.2), channel_id=1, replica_groups=mesh['shot'=4,'rcv'=8] {'rcv'}, dimensions={1}, use_global_device_ids=true | all-gather | bytes 589824 | tf_op jit(solution)/shard_map/all_gather | solution.py:38
  42.1 2.9 rev.3
  45.0 0.1 pad.7.clone
  45.1 0.9 maximum_maximum_fusion
  46.0 1.3 copy.14
  47.3 28.0 %tile.4 = bf16[64,129,32,128]{3,2,1,0:T(8,128)(2,1)} broadcast(bf16[129,32,128]{2,1,0:T(8,128)(2,1)S(1)} %copy.14), dimensions={1,2,3} | broadcast | bytes 68689920 | tf_op jit(solution)/shard_map/tile | solution.py:15
  75.3 44.3 %slice.14 = bf16[8192,32,128]{2,1,0:T(8,128)(2,1)} slice(bf16[8256,32,128]{2,1,0:T(8,128)(2,1)} %bitcast.4), slice={[0:8192], [0:32], [0:128]} | slice | bytes 134217728 | tf_op jit(solution)/shard_map/slice | solution.py:15
  119.6 150.2 %copy.19 = bf16[64,128,32,128]{1,0,3,2:T(8,128)(2,1)} copy(bf16[64,128,32,128]{3,2,1,0:T(8,128)(2,1)} %bitcast.5) | data formatting | bytes 134217728 | tf_op jit(solution)/shard_map/reshape | solution.py:16
  269.8 0.0 all-gather.2.cloned.1.call-done
  269.8 1.9 copy.11
  271.7 0.1 pad.4
  271.8 0.5 fusion.14
  272.3 2.0 copy.21
  274.4 0.0 copy-start
  274.4 2.1 copy.20
  276.4 0.0 copy-done
  276.4 38.1 %fusion.10 = bf16[32,8,8,64]{3,2,0,1:T(8,128)(2,1)S(1)} fusion(bf16[64,128,32,128]{1,0,3,2:T(8,128)(2,1)} %copy.19, bf16[128,8,8,64]{3,2,0,1:T(8,128)(2,1)S(1)} %copy-done, bf16[128,8,8,64]{3,2,0,1:T(8,128)(2,1)} %copy.20), kind=kOutput, calls=%fused_computation.8 | convolution fusion | flops 4299292672 | bytes 69468160 | tf_op jit(solution)/shard_map/uvsk,krbv->srbu/dot_general | solution.py:30
  314.5 0.3 convert_element_type.13
  314.8 0.9 copy.16
  (2 shorter events, 0.0 us)
Async XLA Ops:
  6.5 263.3 %all-gather.2.cloned.1.call-start = ((), (), s32[]{:S(2)}) async-start(), calls=%async_computation | async-start | bytes 1310720 | tf_op jit(solution)/shard_map/all_gather | solution.py:39
  274.4 2.1 copy-start
Sparse Core Ops, SparseCore 0:
  8.9 19.4 all-gather.1
where the time goes:
time: 324 us; the launch traced here: 323 us
  local copies, waits for them, and re-layouts  235 us (73%)
  matrix products  38.1 us (12%)
  blocking collectives  34.9 us (11%)
  between operations  13.5 us (4%)
    reshape x1, local copies, waits for them, and re-layouts, banded(): return repeated.reshape(tap_count, 2 * tap_count, shots_here, rows_in)  150 us
    slice x1, local copies, waits for them, and re-layouts, banded(): repeated = jnp.tile(pattern, (tap_count, 1, 1))[:2 * tap_count * tap_count]  44.3 us
    dot_general x1, matrix products, contract(): jnp.einsum('uvsk,krbv->srbu', band, windows, preferred_element_type=jnp.f...  38.1 us
    all_gather x1, blocking collectives, shards(): responses_all = lax.all_gather(response, 'rcv', axis=1, tiled=True)  34.9 us
    another operation x1, local copies, waits for them, and re-layouts, banded(): repeated = jnp.tile(pattern, (tap_count, 1, 1))[:2 * tap_count * tap_count]  28 us
  transfers between devices with their start and end apart: 1, of which 0 were waited for; matrix products, arithmetic and copies ran while one was open for 71% of the time, Pallas kernels for 0%

commit v1 on v0

v1 whole, which is shorter than its diff:
```python
import functools

import jax
import jax.numpy as jnp
from jax import lax
from jax.experimental import pallas as pl
from jax.experimental.pallas import tpu as pltpu
from jax.sharding import PartitionSpec as P

MESH = pl.DeviceIdType.MESH
LANES = 128
WIDTH = 256


def put(ref, value):
    for t in range(value.shape[1] // LANES):
        ref[t] = value[:, t * LANES : (t + 1) * LANES]


def put_rows(ref, start, count, stride, value):
    for t in range(value.shape[1] // LANES):
        ref[t, pl.ds(start, count, stride=stride), :] = value[:, t * LANES : (t + 1) * LANES]


def get(ref):
    return jnp.concatenate([ref[t] for t in range(ref.shape[0])], axis=1)


def get_rows(ref, start, count, stride):
    return jnp.concatenate(
        [ref[t, pl.ds(start, count, stride=stride), :] for t in range(ref.shape[0])], axis=1
    )


def prepare(response_ref, traces_ref, x_ref, g_ref, a_ref, z_ref, w_ref, b_ref, y_ref, h_ref):
    shots, rows_e, taps = response_ref.shape
    rows_d, rcv, samples = traces_ref.shape
    phases = WIDTH // shots
    blocks = samples // phases
    per_tile = LANES // shots
    tiles = taps // per_tile

    b_ref[:, :taps] = response_ref[...].astype(jnp.float32).reshape(shots * rows_e, taps)
    stacked = jnp.concatenate(
        [b_ref[pl.ds(k, shots, stride=rows_e), :] for k in range(rows_e)], axis=0
    )
    put(y_ref, stacked.T[:taps])
    by_tap = [get_rows(y_ref, m, tiles, per_tile) for m in range(per_tile)]
    for k in range(rows_e):
        h_ref[pl.ds(k, tiles, stride=rows_e), :] = jnp.concatenate(
            [v[:, k * shots : (k + 1) * shots] for v in by_tap], axis=1
        )
    g_ref[...] = h_ref[...].astype(jnp.bfloat16)

    put(a_ref, traces_ref[...].astype(jnp.float32).reshape(rows_d * rcv, samples))
    stacked = jnp.concatenate([get_rows(a_ref, r, rows_d, rcv) for r in range(rcv)], axis=0)
    put(z_ref, stacked.T)
    by_phase = [get_rows(z_ref, v, blocks, phases) for v in range(phases)]
    for r in range(rcv):
        row = jnp.concatenate([z[:, r * rows_d : (r + 1) * rows_d] for z in by_phase], axis=1)
        put_rows(w_ref, r, blocks, rcv, row)
    x_ref[...] = get(w_ref).astype(jnp.bfloat16)


def predict(
    n_shot, n_rcv, chunks, taps, shots, rcv, samples,
    x_ref, g_ref, o_ref,
    xland, gland, bands, even, odd, acc, z_ref, f_ref,
    xsend, xrecv, xfwd, gsend, grecv, gfwd,
):
    rows, width = x_ref.shape
    phases = WIDTH // shots
    blocks = samples // phases
    per_tile = LANES // shots
    tiles = taps // per_tile
    pad = phases // per_tile
    rows_d = width // phases
    rows_e = g_ref.shape[0] // tiles
    history = taps // phases
    ratio = rows_d // rows_e
    outer_d, outer_e = n_shot // 2, n_rcv // 2
    me_d, me_e = lax.axis_index("shot"), lax.axis_index("rcv")
    in_d, in_e = lax.rem(me_d, 2), lax.rem(me_e, 2)
    out_d, out_e = me_d // 2, me_e // 2
    mate_d = out_d * 2 + 1 - in_d
    mate_e = out_e * 2 + 1 - in_e

    def at_d(step):
        return lax.rem(out_d + step + outer_d, outer_d) * 2 + in_d

    def at_e(step):
        return lax.rem(out_e + step + outer_e, outer_e) * 2 + in_e

    barrier = pltpu.get_barrier_semaphore()
    peers = [(mate_d, me_e), (me_d, mate_e)]
    peers += [(at_d(i), me_e) for i in range(1, outer_d)]
    peers += [(me_d, at_e(i)) for i in range(1, outer_e)]
    for peer in peers:
        pl.semaphore_signal(barrier, inc=1, device_id=peer, device_id_type=MESH)
    pl.semaphore_wait(barrier, len(peers))

    part = rows // chunks

    def xcopy(src, owner, c, send, peer):
        piece = pl.ds(c * part, part)
        return pltpu.make_async_remote_copy(
            src_ref=src.at[piece],
            dst_ref=xland.at[owner, piece],
            send_sem=send,
            recv_sem=xrecv.at[owner, c],
            device_id=peer,
            device_id_type=MESH,
        )

    def gcopy(src, owner, send, peer):
        return pltpu.make_async_remote_copy(
            src_ref=src,
            dst_ref=gland.at[owner],
            send_sem=send,
            recv_sem=grecv.at[owner],
            device_id=peer,
            device_id_type=MESH,
        )

    pending = []

    def go(copy):
        copy.start()
        pending.append(copy)

    for i in range(1, outer_e):
        go(gcopy(g_ref, me_e, gsend.at[i], (me_d, at_e(i))))
    go(gcopy(g_ref, me_e, gsend.at[0], (me_d, mate_e)))
    for c in range(chunks):
        for i in range(1, outer_d):
            go(xcopy(x_ref, me_d, c, xsend.at[i, c], (at_d(i), me_e)))
    for c in range(chunks):
        go(xcopy(x_ref, me_d, c, xsend.at[0, c], (mate_d, me_e)))

    todo_g = [at_e(-i) for i in range(1, outer_e)]
    todo_x = [(i, at_d(-i), c) for c in range(chunks) for i in range(1, outer_d)]
    for n in range(max(len(todo_g), len(todo_x))):
        if n < len(todo_g):
            owner = todo_g[n]
            gcopy(gland.at[owner], owner, gfwd.at[n], (me_d, mate_e)).wait_recv()
            go(gcopy(gland.at[owner], owner, gfwd.at[n], (me_d, mate_e)))
        if n < len(todo_x):
            i, owner, c = todo_x[n]
            copy = xcopy(xland.at[owner], owner, c, xfwd.at[i, c], (mate_d, me_e))
            copy.wait_recv()
            go(copy)
    for i in range(outer_e):
        owner = lax.rem(out_e + i, outer_e) * 2 + 1 - in_e
        gcopy(g_ref, owner, gsend.at[0], (me_d, mate_e)).wait_recv()
    gland[me_e] = g_ref[...]

    blank = jnp.zeros((rows_e, LANES), jnp.bfloat16)
    for e in range(n_rcv):
        place = pl.ds((e % ratio) * rows_e, rows_e)
        held = gland[e]
        padded = [blank] * pad
        padded += [held[a * rows_e : (a + 1) * rows_e] for a in range(tiles)]
        padded += [blank] * (pad + 1)
        for a in range(tiles + 2 * pad):
            for q in range(per_tile):
                value = padded[a]
                if q > 0:
                    value = jnp.concatenate(
                        [padded[a][:, q * shots :], padded[a + 1][:, : q * shots]], axis=1
                    )
                bands[e // ratio, q, a, place, :] = value

    head = history * rcv
    even[pl.ds(0, head), :] = jnp.zeros((head, width), jnp.bfloat16)
    odd[pl.ds(0, head), :] = jnp.zeros((head, width), jnp.bfloat16)

    def add(owner, held, first):
        even[pl.ds(head, rows), :] = held
        odd[pl.ds(head - rcv, rows), :] = held
        left, right = [], []
        for v1 in range(history + 1):
            if v1 % 2 == 0:
                left.append(even[pl.ds(v1 * rcv, rows), :])
            else:
                left.append(odd[pl.ds((v1 - 1) * rcv, rows), :])
            for v0 in range(phases):
                start = taps - v1 * phases - v0 + phases
                a, q = start // per_tile, start % per_tile
                right.append(
                    jnp.concatenate([bands[owner, q, a + n] for n in range(pad)], axis=1)
                )
        product = jnp.dot(
            jnp.concatenate(left, axis=1),
            jnp.concatenate(right, axis=0),
            preferred_element_type=jnp.float32,
        )
        put(acc, product if first else get(acc) + product)

    add(me_d, x_ref[...], True)
    for step in range(outer_d):
        owners = [lax.rem(out_d + step, outer_d) * 2 + 1 - in_d]
        if step > 0:
            owners = [at_d(step)] + owners
        for n, owner in enumerate(owners):
            if step == 0 or n == 1:
                for c in range(chunks):
                    xcopy(x_ref, owner, c, xsend.at[0, c], (mate_d, me_e)).wait_recv()
            add(owner, xland[owner], False)

    by_rcv = [get_rows(acc, r, blocks, rcv) for r in range(rcv)]
    for u in range(phases):
        row = jnp.concatenate([v[:, u * shots : (u + 1) * shots] for v in by_rcv], axis=1)
        put_rows(z_ref, u, blocks, phases, row)
    turned = get(z_ref).T
    for r in range(rcv):
        put_rows(f_ref, r, shots, rcv, turned[r * shots : (r + 1) * shots])
    o_ref[...] = get(f_ref).reshape(shots, rcv, samples).astype(jnp.bfloat16)
    for copy in pending:
        copy.wait_send()


def shards(n_shot, n_rcv, response, traces):
    shots, rows_e, taps = response.shape
    rows_d, rcv, samples = traces.shape
    phases = WIDTH // shots
    blocks = samples // phases
    per_tile = LANES // shots
    tiles = taps // per_tile
    pad = phases // per_tile
    rows = blocks * rcv
    width = phases * rows_d
    chunks = 4
    f32, bf16 = jnp.float32, jnp.bfloat16

    def tiled(height, across):
        return pltpu.VMEM((across // LANES, height, LANES), f32)

    vmem = pl.BlockSpec(memory_space=pltpu.VMEM)
    x, g = pl.pallas_call(
        prepare,
        out_shape=(
            jax.ShapeDtypeStruct((rows, width), bf16),
            jax.ShapeDtypeStruct((tiles * rows_e, LANES), bf16),
        ),
        in_specs=[vmem] * 2,
        out_specs=(vmem, vmem),
        scratch_shapes=[
            tiled(rows_d * rcv, samples),
            tiled(samples, rcv * rows_d),
            tiled(rows, width),
            pltpu.VMEM((shots * rows_e, LANES), f32),
            tiled(taps, rows_e * shots),
            pltpu.VMEM((tiles * rows_e, LANES), f32),
        ],
    )(response, traces)
    outer_d, outer_e = n_shot // 2, n_rcv // 2
    head = taps // phases * rcv
    dma = pltpu.SemaphoreType.DMA
    return pl.pallas_call(
        functools.partial(predict, n_shot, n_rcv, chunks, taps, shots, rcv, samples),
        out_shape=jax.ShapeDtypeStruct((shots, rcv, samples), bf16),
        in_specs=[vmem] * 2,
        out_specs=vmem,
        scratch_shapes=[
            pltpu.VMEM((n_shot, rows, width), bf16),
            pltpu.VMEM((n_rcv, tiles * rows_e, LANES), bf16),
            pltpu.VMEM((n_shot, per_tile, tiles + 2 * pad, rows_d, LANES), bf16),
            pltpu.VMEM((rows + head, width), bf16),
            pltpu.VMEM((rows + head, width), bf16),
            tiled(rows, WIDTH),
            tiled(samples, rcv * shots),
            tiled(shots * rcv, samples),
            dma((outer_d, chunks)),
            dma((n_shot, chunks)),
            dma((outer_d, chunks)),
            dma((outer_e,)),
            dma((n_rcv,)),
            dma((outer_e,)),
        ],
        compiler_params=pltpu.CompilerParams(collective_id=0, has_side_effects=True),
    )(x, g)


def solution(mesh):
    placed = P("shot", "rcv", None)
    return jax.shard_map(
        functools.partial(shards, mesh.shape["shot"], mesh.shape["rcv"]),
        mesh=mesh, in_specs=(placed, placed), out_specs=placed, check_vma=False,
    )
```

time: 324 us -> 26.8 us (0.08)
  local copies, waits for them, and re-layouts: 235 us -> 1.67 us
  matrix products: 38.1 us -> 0 us
  blocking collectives: 34.9 us -> 0 us
  Pallas kernels: 0 us -> 25 us
  between operations: 13.5 us -> 0.01 us
    reshape x1 -> x0, local copies, waits for them, and re-layouts: 150 us -> none  [banded(): return repeated.reshape(tap_count, 2 * tap_count, shots_here, rows_in)]
    slice x2 -> x0, local copies, waits for them, and re-layouts: 44.8 us -> none  [the longest x1 44.3 us: banded(): repeated = jnp.tile(pattern, (tap_count, 1, 1))[:2 * tap_count * tap_count]]
    dot_general x1 -> x0, matrix products: 38.1 us -> none  [contract(): jnp.einsum('uvsk,krbv->srbu', band, windows, preferred_element_type=jnp.f...]
    all_gather x1 -> x0, blocking collectives: 34.9 us -> none  [shards(): responses_all = lax.all_gather(response, 'rcv', axis=1, tiled=True)]
    another operation x1 -> x0, local copies, waits for them, and re-layouts: 28 us -> none  [banded(): repeated = jnp.tile(pattern, (tap_count, 1, 1))[:2 * tap_count * tap_count]]
    pallas_call x0 -> x2, Pallas kernels: none -> 25 us  [the longest x1 22.4 us: shards(): pl.pallas_call(functools.partial(predict, n_shot, n_rcv, chunks, taps, sh...]
  transfers between devices with their start and end apart: 1 -> 0, of which waited for: 0 -> 0; matrix products, arithmetic and copies ran while one was open for 71% -> 0% of each run, Pallas kernels for 0% -> 0%
where the time goes in v1:
time: 26.8 us; the launch traced here: 26.7 us
  Pallas kernels  25 us (93%)
  local copies, waits for them, and re-layouts  1.67 us (6%)
    pallas_call x1, Pallas kernels, shards(): pl.pallas_call(functools.partial(predict, n_shot, n_rcv, chunks, taps, sh...  22.4 us
    pallas_call x1, Pallas kernels, shards(): pl.pallas_call(prepare, out_shape=(jax.ShapeDtypeStruct((rows, width), bf...  2.6 us
    unnamed x1, local copies, waits for them, and re-layouts  1.67 us

profile of v1, /device:TPU:0, one launch (start us, length us, event | category | flops | bytes accessed | tf_op | source)
XLA Modules:
  0.0 26.7 jit_solution(8628019817787706888)
XLA Ops:
  0.0 2.6 %shard_map.28 = (bf16[512,256]{1,0:T(8,128)(2,1)}, bf16[256,128]{1,0:T(8,128)(2,1)}) custom-call(bf16[32,16,64]{2,1,0:T(8,128)(2,1)} %response_ref.1, bf16[32,8,512]{2,1,0:T(8,128)(2,1)} %traces_ref.1), custom_call_target="tpu_custom_call" | custom-call | tf_op jit(solution)/shard_map/pallas_call | solution.py:239
  2.6 22.4 %shard_map.29 = bf16[32,8,512]{2,1,0:T(8,128)(2,1)} custom-call(bf16[512,256]{1,0:T(8,128)(2,1)} %get-tuple-element.7.x_ref, bf16[256,128]{1,0:T(8,128)(2,1)} %get-tuple-element.8.g_ref), custom_call_target="tpu_custom_call" | custom-call | tf_op jit(solution)/shard_map/pallas_call | solution.py:259
  25.0 1.7 %copy.4 = bf16[32,8,512]{2,1,0:T(8,128)(2,1)} copy(bf16[32,8,512]{2,1,0:T(8,128)(2,1)} %shard_map.29) | data formatting | bytes 524288

commit v2 on v1

v2 whole, which is shorter than its diff:
```python
import functools

import jax
import jax.numpy as jnp
from jax import lax
from jax.experimental import pallas as pl
from jax.experimental.pallas import tpu as pltpu
from jax.sharding import PartitionSpec as P

MESH = pl.DeviceIdType.MESH
LANES = 128
WIDTH = 256


def put(ref, value):
    for t in range(value.shape[1] // LANES):
        ref[t] = value[:, t * LANES : (t + 1) * LANES]


def put_rows(ref, start, count, stride, value):
    for t in range(value.shape[1] // LANES):
        ref[t, pl.ds(start, count, stride=stride), :] = value[:, t * LANES : (t + 1) * LANES]


def get(ref):
    return jnp.concatenate([ref[t] for t in range(ref.shape[0])], axis=1)


def get_rows(ref, start, count, stride):
    return jnp.concatenate(
        [ref[t, pl.ds(start, count, stride=stride), :] for t in range(ref.shape[0])], axis=1
    )


def turn_response(response, b_ref, y_ref, h_ref):
    shots, rows_e, taps = response.shape
    per_tile = LANES // shots
    tiles = taps // per_tile
    b_ref[:, :taps] = response.astype(jnp.float32).reshape(shots * rows_e, taps)
    stacked = jnp.concatenate(
        [b_ref[pl.ds(k, shots, stride=rows_e), :] for k in range(rows_e)], axis=0
    )
    put(y_ref, stacked.T[:taps])
    by_tap = [get_rows(y_ref, m, tiles, per_tile) for m in range(per_tile)]
    for k in range(rows_e):
        h_ref[pl.ds(k, tiles, stride=rows_e), :] = jnp.concatenate(
            [v[:, k * shots : (k + 1) * shots] for v in by_tap], axis=1
        )
    return h_ref[...].astype(jnp.bfloat16)


def turn_traces(traces, phases, a_ref, z_ref, w_ref):
    rows_d, rcv, samples = traces.shape
    blocks = samples // phases
    put(a_ref, traces.astype(jnp.float32).reshape(rows_d * rcv, samples))
    stacked = jnp.concatenate([get_rows(a_ref, r, rows_d, rcv) for r in range(rcv)], axis=0)
    put(z_ref, stacked.T)
    by_phase = [get_rows(z_ref, v, blocks, phases) for v in range(phases)]
    for r in range(rcv):
        row = jnp.concatenate([z[:, r * rows_d : (r + 1) * rows_d] for z in by_phase], axis=1)
        put_rows(w_ref, r, blocks, rcv, row)
    return get(w_ref).astype(jnp.bfloat16)


def arrange(y_ref, o_ref, acc, z_ref, f_ref):
    shots, rcv, samples = o_ref.shape
    phases = WIDTH // shots
    blocks = samples // phases
    put(acc, y_ref[...].astype(jnp.float32))
    by_rcv = [get_rows(acc, r, blocks, rcv) for r in range(rcv)]
    for u in range(phases):
        row = jnp.concatenate([v[:, u * shots : (u + 1) * shots] for v in by_rcv], axis=1)
        put_rows(z_ref, u, blocks, phases, row)
    turned = get(z_ref).T
    for r in range(rcv):
        put_rows(f_ref, r, shots, rcv, turned[r * shots : (r + 1) * shots])
    o_ref[...] = get(f_ref).reshape(shots, rcv, samples).astype(jnp.bfloat16)


def predict(
    n_shot, n_rcv, chunks,
    response_hbm, traces_hbm, o_ref,
    response_ref, traces_ref, b_ref, y_ref, h_ref, a_ref, z_ref, w_ref,
    x_ref, g_ref, xland, gland, bands, even, odd, acc,
    load, xsend, xrecv, xfwd, gsend, grecv, gfwd,
):
    shots, rows_e, taps = response_ref.shape
    rows_d, rcv, samples = traces_ref.shape
    rows, width = x_ref.shape
    phases = WIDTH // shots
    per_tile = LANES // shots
    tiles = taps // per_tile
    pad = phases // per_tile
    history = taps // phases
    ratio = rows_d // rows_e
    head = history * rcv
    half = rows // 2
    outer_d, outer_e = n_shot // 2, n_rcv // 2
    me_d, me_e = lax.axis_index("shot"), lax.axis_index("rcv")
    in_d, in_e = lax.rem(me_d, 2), lax.rem(me_e, 2)
    out_d, out_e = me_d // 2, me_e // 2
    mate_d = out_d * 2 + 1 - in_d
    mate_e = out_e * 2 + 1 - in_e

    def at_d(step):
        return lax.rem(out_d + step + outer_d, outer_d) * 2 + in_d

    def at_e(step):
        return lax.rem(out_e + step + outer_e, outer_e) * 2 + in_e

    barrier = pltpu.get_barrier_semaphore()
    peers = [(mate_d, me_e), (me_d, mate_e)]
    peers += [(at_d(i), me_e) for i in range(1, outer_d)]
    peers += [(me_d, at_e(i)) for i in range(1, outer_e)]
    for peer in peers:
        pl.semaphore_signal(barrier, inc=1, device_id=peer, device_id_type=MESH)
    fetch_r = pltpu.make_async_copy(response_hbm, response_ref, load.at[0])
    fetch_t = pltpu.make_async_copy(traces_hbm, traces_ref, load.at[1])
    fetch_r.start()
    fetch_t.start()

    part = rows // chunks

    def xcopy(src, owner, c, send, peer):
        piece = pl.ds(c * part, part)
        return pltpu.make_async_remote_copy(
            src_ref=src.at[piece],
            dst_ref=xland.at[owner, piece],
            send_sem=send,
            recv_sem=xrecv.at[owner, c],
            device_id=peer,
            device_id_type=MESH,
        )

    def gcopy(src, owner, send, peer):
        return pltpu.make_async_remote_copy(
            src_ref=src,
            dst_ref=gland.at[owner],
            send_sem=send,
            recv_sem=grecv.at[owner],
            device_id=peer,
            device_id_type=MESH,
        )

    pending = []

    def go(copy):
        copy.start()
        pending.append(copy)

    fetch_r.wait()
    g_ref[...] = turn_response(response_ref[...], b_ref, y_ref, h_ref)
    pl.semaphore_wait(barrier, len(peers))
    for i in range(1, outer_e):
        go(gcopy(g_ref, me_e, gsend.at[i], (me_d, at_e(i))))
    go(gcopy(g_ref, me_e, gsend.at[0], (me_d, mate_e)))
    fetch_t.wait()
    x_ref[...] = turn_traces(traces_ref[...], phases, a_ref, z_ref, w_ref)
    for c in range(chunks):
        for i in range(1, outer_d):
            go(xcopy(x_ref, me_d, c, xsend.at[i, c], (at_d(i), me_e)))
    for c in range(chunks):
        go(xcopy(x_ref, me_d, c, xsend.at[0, c], (mate_d, me_e)))

    blank = jnp.zeros((rows_e, LANES), jnp.bfloat16)

    def build(e, held):
        padded = [blank] * pad
        padded += [held[a * rows_e : (a + 1) * rows_e] for a in range(tiles)]
        padded += [blank] * (pad + 1)
        for a in range(tiles + 2 * pad):
            for q in range(per_tile):
                value = padded[a]
                if q > 0:
                    value = jnp.concatenate(
                        [padded[a][:, q * shots :], padded[a + 1][:, : q * shots]], axis=1
                    )
                bands[e, q, a] = value

    def place(owner, held, h):
        even[owner, pl.ds(head + h * half, half), :] = held
        odd[owner, pl.ds(head - rcv + h * half, half), :] = held

    def add(owner, h, first=False, last=False):
        left, right = [], []
        for v1 in range(history + 1):
            if v1 % 2 == 0:
                left.append(even[owner, pl.ds(h * half + v1 * rcv, half), :])
            else:
                left.append(odd[owner, pl.ds(h * half + (v1 - 1) * rcv, half), :])
            for v0 in range(phases):
                start = taps - v1 * phases - v0 + phases
                a, q = start // per_tile, start % per_tile
                for k in range(ratio):
                    e = owner * ratio + k
                    right.append(
                        jnp.concatenate([bands[e, q, a + n] for n in range(pad)], axis=1)
                    )
        total = jnp.dot(
            jnp.concatenate(left, axis=1),
            jnp.concatenate(right, axis=0),
            preferred_element_type=jnp.float32,
        )
        mine = pl.ds(h * half, half)
        if not first:
            total = acc[mine, :] + total
        if last:
            o_ref[mine, :] = total.astype(jnp.bfloat16)
        else:
            acc[mine, :] = total

    def forward_x(i, c):
        owner = at_d(-i)
        copy = xcopy(xland.at[owner], owner, c, xfwd.at[i, c], (mate_d, me_e))
        copy.wait_recv()
        go(copy)

    for d in range(n_shot):
        even[d, pl.ds(0, head), :] = jnp.zeros((head, width), jnp.bfloat16)
        odd[d, pl.ds(0, head), :] = jnp.zeros((head, width), jnp.bfloat16)
    for h in range(2):
        place(me_d, x_ref[pl.ds(h * half, half), :], h)
    build(me_e, g_ref[...])

    todo = [(i, c) for c in range(chunks) for i in range(1, outer_d)]
    late = [t for t in todo if t[1] == chunks - 1]
    todo = [t for t in todo if t[1] < chunks - 1]
    for n in range(max(outer_e - 1, len(todo))):
        if n < outer_e - 1:
            owner = at_e(-n - 1)
            copy = gcopy(gland.at[owner], owner, gfwd.at[n], (me_d, mate_e))
            copy.wait_recv()
            go(copy)
        if n < len(todo):
            forward_x(*todo[n])
        if n < outer_e - 1:
            build(owner, gland[owner])
    for i in range(outer_e):
        owner = lax.rem(out_e - i + outer_e, outer_e) * 2 + 1 - in_e
        gcopy(g_ref, owner, gsend.at[0], (me_d, mate_e)).wait_recv()
        build(owner, gland[owner])

    def arrived(owner, h):
        for c in range(h * chunks // 2, (h + 1) * chunks // 2):
            xcopy(x_ref, owner, c, xsend.at[0, c], (mate_d, me_e)).wait_recv()

    def bring(owner, h):
        place(owner, xland[owner, pl.ds(h * half, half), :], h)

    add(me_d, 0, first=True)
    for t in late:
        forward_x(*t)
    add(me_d, 1, first=True)
    for h in range(2):
        arrived(mate_d, h)
        bring(mate_d, h)
        add(mate_d, h)
    for h in range(2):
        for i in range(1, outer_d):
            bring(at_d(-i), h)
            add(at_d(-i), h)
        for i in range(1, outer_d):
            owner = lax.rem(out_d - i + outer_d, outer_d) * 2 + 1 - in_d
            arrived(owner, h)
            bring(owner, h)
            add(owner, h, last=i == outer_d - 1)
    for copy in pending:
        copy.wait_send()


def shards(n_shot, n_rcv, response, traces):
    shots, rows_e, taps = response.shape
    rows_d, rcv, samples = traces.shape
    phases = WIDTH // shots
    blocks = samples // phases
    per_tile = LANES // shots
    tiles = taps // per_tile
    pad = phases // per_tile
    rows = blocks * rcv
    width = phases * rows_d
    chunks = 4
    f32, bf16 = jnp.float32, jnp.bfloat16

    def tiled(height, across):
        return pltpu.VMEM((across // LANES, height, LANES), f32)

    vmem = pl.BlockSpec(memory_space=pltpu.VMEM)
    outer_d, outer_e = n_shot // 2, n_rcv // 2
    head = taps // phases * rcv
    dma = pltpu.SemaphoreType.DMA
    y = pl.pallas_call(
        functools.partial(predict, n_shot, n_rcv, chunks),
        out_shape=jax.ShapeDtypeStruct((rows, WIDTH), bf16),
        in_specs=[pl.BlockSpec(memory_space=pl.ANY)] * 2,
        out_specs=vmem,
        scratch_shapes=[
            pltpu.VMEM(response.shape, bf16),
            pltpu.VMEM(traces.shape, bf16),
            pltpu.VMEM((shots * rows_e, LANES), f32),
            tiled(taps, rows_e * shots),
            pltpu.VMEM((tiles * rows_e, LANES), f32),
            tiled(rows_d * rcv, samples),
            tiled(samples, rcv * rows_d),
            tiled(rows, width),
            pltpu.VMEM((rows, width), bf16),
            pltpu.VMEM((tiles * rows_e, LANES), bf16),
            pltpu.VMEM((n_shot, rows, width), bf16),
            pltpu.VMEM((n_rcv, tiles * rows_e, LANES), bf16),
            pltpu.VMEM((n_rcv, per_tile, tiles + 2 * pad, rows_e, LANES), bf16),
            pltpu.VMEM((n_shot, rows + head, width), bf16),
            pltpu.VMEM((n_shot, rows + head, width), bf16),
            pltpu.VMEM((rows, WIDTH), f32),
            dma((2,)),
            dma((outer_d, chunks)),
            dma((n_shot, chunks)),
            dma((outer_d, chunks)),
            dma((outer_e,)),
            dma((n_rcv,)),
            dma((outer_e,)),
        ],
        compiler_params=pltpu.CompilerParams(collective_id=0, has_side_effects=True),
    )(response, traces)
    return pl.pallas_call(
        arrange,
        out_shape=jax.ShapeDtypeStruct((shots, rcv, samples), bf16),
        in_specs=[vmem],
        out_specs=vmem,
        scratch_shapes=[
            tiled(rows, WIDTH),
            tiled(samples, rcv * shots),
            tiled(shots * rcv, samples),
        ],
    )(y)


def solution(mesh):
    placed = P("shot", "rcv", None)
    return jax.shard_map(
        functools.partial(shards, mesh.shape["shot"], mesh.shape["rcv"]),
        mesh=mesh, in_specs=(placed, placed), out_specs=placed, check_vma=False,
    )
```

time: 26.8 us -> 23.5 us (0.88)
  Pallas kernels: 25 us -> 23.3 us
  local copies, waits for them, and re-layouts: 1.67 us -> 0 us
    pallas_call x2, Pallas kernels: 25 us -> 23.3 us  [the longest x1 20.9 us: shards(): pl.pallas_call(functools.partial(predict, n_shot, n_rcv, chunks), out_sha...]
    unnamed x1 -> x0, local copies, waits for them, and re-layouts: 1.67 us -> none
where the time goes in v2:
time: 23.5 us; the launch traced here: 23.3 us
  Pallas kernels  23.3 us (99%)
    pallas_call x1, Pallas kernels, shards(): pl.pallas_call(functools.partial(predict, n_shot, n_rcv, chunks), out_sha...  20.9 us
    pallas_call x1, Pallas kernels, shards(): pl.pallas_call(arrange, out_shape=jax.ShapeDtypeStruct((shots, rcv, sampl...  2.38 us

profile of v2, /device:TPU:0, one launch (start us, length us, event | category | flops | bytes accessed | tf_op | source)
XLA Modules:
  0.0 23.3 jit_solution(3007543983559720930)
XLA Ops:
  0.0 20.9 %shard_map.28.y_ref = bf16[512,256]{1,0:T(8,128)(2,1)} custom-call(bf16[32,16,64]{2,1,0:T(8,128)(2,1)} %response_hbm.1, bf16[32,8,512]{2,1,0:T(8,128)(2,1)} %traces_hbm.1), custom_call_target="tpu_custom_call" | custom-call | tf_op jit(solution)/shard_map/pallas_call | solution.py:291
  20.9 2.4 %shard_map.29 = bf16[32,8,512]{2,1,0:T(8,128)(2,1)} custom-call(bf16[512,256]{1,0:T(8,128)(2,1)} %shard_map.28.y_ref), custom_call_target="tpu_custom_call" | custom-call | tf_op jit(solution)/shard_map/pallas_call | solution.py:323

commit v3 on v2

--- a/solution.py
+++ b/solution.py
@@ -151,7 +151,8 @@
     fetch_r.wait()
     g_ref[...] = turn_response(response_ref[...], b_ref, y_ref, h_ref)
     pl.semaphore_wait(barrier, len(peers))
-    for i in range(1, outer_e):
+    order = sorted(range(1, outer_e), key=lambda i: abs(2 * i - outer_e))
+    for i in order:
         go(gcopy(g_ref, me_e, gsend.at[i], (me_d, at_e(i))))
     go(gcopy(g_ref, me_e, gsend.at[0], (me_d, mate_e)))
     fetch_t.wait()
@@ -222,12 +223,18 @@
         place(me_d, x_ref[pl.ds(h * half, half), :], h)
     build(me_e, g_ref[...])
 
+    def arrived(owner):
+        for c in range(chunks):
+            xcopy(x_ref, owner, c, xsend.at[0, c], (mate_d, me_e)).wait_recv()
+
+    def bring(owner):
+        for h in range(2):
+            place(owner, xland[owner, pl.ds(h * half, half), :], h)
+
     todo = [(i, c) for c in range(chunks) for i in range(1, outer_d)]
-    late = [t for t in todo if t[1] == chunks - 1]
-    todo = [t for t in todo if t[1] < chunks - 1]
     for n in range(max(outer_e - 1, len(todo))):
         if n < outer_e - 1:
-            owner = at_e(-n - 1)
+            owner = at_e(-order[n])
             copy = gcopy(gland.at[owner], owner, gfwd.at[n], (me_d, mate_e))
             copy.wait_recv()
             go(copy)
@@ -235,35 +242,27 @@
             forward_x(*todo[n])
         if n < outer_e - 1:
             build(owner, gland[owner])
-    for i in range(outer_e):
-        owner = lax.rem(out_e - i + outer_e, outer_e) * 2 + 1 - in_e
+    arrived(mate_d)
+    bring(mate_d)
+    for i in range(1, outer_d):
+        bring(at_d(-i))
+    for i in range(1, outer_d):
+        owner = lax.rem(out_d - i + outer_d, outer_d) * 2 + 1 - in_d
+        arrived(owner)
+        bring(owner)
+
+    for n, i in enumerate([0] + order):
+        group = lax.rem(out_e - i + outer_e, outer_e)
+        owner = group * 2 + 1 - in_e
         gcopy(g_ref, owner, gsend.at[0], (me_d, mate_e)).wait_recv()
         build(owner, gland[owner])
-
-    def arrived(owner, h):
-        for c in range(h * chunks // 2, (h + 1) * chunks // 2):
-            xcopy(x_ref, owner, c, xsend.at[0, c], (mate_d, me_e)).wait_recv()
-
-    def bring(owner, h):
-        place(owner, xland[owner, pl.ds(h * half, half), :], h)
-
-    add(me_d, 0, first=True)
-    for t in late:
-        forward_x(*t)
-    add(me_d, 1, first=True)
-    for h in range(2):
-        arrived(mate_d, h)
-        bring(mate_d, h)
-        add(mate_d, h)
-    for h in range(2):
-        for i in range(1, outer_d):
-            bring(at_d(-i), h)
-            add(at_d(-i), h)
-        for i in range(1, outer_d):
-            owner = lax.rem(out_d - i + outer_d, outer_d) * 2 + 1 - in_d
-            arrived(owner, h)
-            bring(owner, h)
-            add(owner, h, last=i == outer_d - 1)
+        if ratio == 2:
+            for h in range(2):
+                add(group, h, first=n == 0, last=n == outer_e - 1)
+    if ratio != 2:
+        for d in range(n_shot):
+            for h in range(2):
+                add(d, h, first=d == 0, last=d == n_shot - 1)
     for copy in pending:
         copy.wait_send()
 

time: 23.5 us -> 21 us (0.89)
  Pallas kernels: 23.3 us -> 20.7 us
    pallas_call x1, Pallas kernels: 20.9 us -> 18.4 us  [shards(): pl.pallas_call(functools.partial(predict, n_shot, n_rcv, chunks), out_sha...]
where the time goes in v3:
time: 21 us; the launch traced here: 20.7 us
  Pallas kernels  20.7 us (99%)
    pallas_call x1, Pallas kernels, shards(): pl.pallas_call(functools.partial(predict, n_shot, n_rcv, chunks), out_sha...  18.4 us
    pallas_call x1, Pallas kernels, shards(): pl.pallas_call(arrange, out_shape=jax.ShapeDtypeStruct((shots, rcv, sampl...  2.38 us

profile of v3, /device:TPU:0, one launch (start us, length us, event | category | flops | bytes accessed | tf_op | source)
XLA Modules:
  0.0 20.7 jit_solution(5325518109122916022)
XLA Ops:
  0.0 18.4 %shard_map.28.y_ref = bf16[512,256]{1,0:T(8,128)(2,1)} custom-call(bf16[32,16,64]{2,1,0:T(8,128)(2,1)} %response_hbm.1, bf16[32,8,512]{2,1,0:T(8,128)(2,1)} %traces_hbm.1), custom_call_target="tpu_custom_call" | custom-call | tf_op jit(solution)/shard_map/pallas_call | solution.py:290
  18.4 2.4 %shard_map.29 = bf16[32,8,512]{2,1,0:T(8,128)(2,1)} custom-call(bf16[512,256]{1,0:T(8,128)(2,1)} %shard_map.28.y_ref), custom_call_target="tpu_custom_call" | custom-call | tf_op jit(solution)/shard_map/pallas_call | solution.py:322

commit v4 on v3

--- a/solution.py
+++ b/solution.py
@@ -156,10 +156,15 @@
         go(gcopy(g_ref, me_e, gsend.at[i], (me_d, at_e(i))))
     go(gcopy(g_ref, me_e, gsend.at[0], (me_d, mate_e)))
     fetch_t.wait()
-    x_ref[...] = turn_traces(traces_ref[...], phases, a_ref, z_ref, w_ref)
-    for c in range(chunks):
-        for i in range(1, outer_d):
-            go(xcopy(x_ref, me_d, c, xsend.at[i, c], (at_d(i), me_e)))
+    span = samples // chunks
+    for c in range(chunks + 1):
+        if c < chunks:
+            x_ref[pl.ds(c * part, part), :] = turn_traces(
+                traces_ref[:, :, pl.ds(c * span, span)], phases, a_ref, z_ref, w_ref
+            )
+        if c > 0:
+            for i in range(1, outer_d):
+                go(xcopy(x_ref, me_d, c - 1, xsend.at[i, c - 1], (at_d(i), me_e)))
     for c in range(chunks):
         go(xcopy(x_ref, me_d, c, xsend.at[0, c], (mate_d, me_e)))
 
@@ -223,15 +228,19 @@
         place(me_d, x_ref[pl.ds(h * half, half), :], h)
     build(me_e, g_ref[...])
 
-    def arrived(owner):
-        for c in range(chunks):
-            xcopy(x_ref, owner, c, xsend.at[0, c], (mate_d, me_e)).wait_recv()
-
-    def bring(owner):
-        for h in range(2):
+    def arrived(h):
+        for i in range(outer_d):
+            owner = lax.rem(out_d - i + outer_d, outer_d) * 2 + 1 - in_d
+            for c in range(h * chunks // 2, (h + 1) * chunks // 2):
+                xcopy(x_ref, owner, c, xsend.at[0, c], (mate_d, me_e)).wait_recv()
             place(owner, xland[owner, pl.ds(h * half, half), :], h)
+            if i > 0:
+                owner = at_d(-i)
+                place(owner, xland[owner, pl.ds(h * half, half), :], h)
 
     todo = [(i, c) for c in range(chunks) for i in range(1, outer_d)]
+    late = todo[len(todo) // 2 :]
+    todo = todo[: len(todo) // 2]
     for n in range(max(outer_e - 1, len(todo))):
         if n < outer_e - 1:
             owner = at_e(-order[n])
@@ -242,24 +251,29 @@
             forward_x(*todo[n])
         if n < outer_e - 1:
             build(owner, gland[owner])
-    arrived(mate_d)
-    bring(mate_d)
-    for i in range(1, outer_d):
-        bring(at_d(-i))
-    for i in range(1, outer_d):
-        owner = lax.rem(out_d - i + outer_d, outer_d) * 2 + 1 - in_d
-        arrived(owner)
-        bring(owner)
-
-    for n, i in enumerate([0] + order):
-        group = lax.rem(out_e - i + outer_e, outer_e)
+    arrived(0)
+
+    groups = [lax.rem(out_e - i + outer_e, outer_e) for i in [0] + order]
+    early = ratio == 2 and outer_e - 1 >= len(late)
+    if not early:
+        for t in late:
+            forward_x(*t)
+    for n, group in enumerate(groups):
+        if early and n == outer_e - 1:
+            arrived(1)
+            for m in range(n):
+                add(groups[m], 1, first=m == 0)
         owner = group * 2 + 1 - in_e
         gcopy(g_ref, owner, gsend.at[0], (me_d, mate_e)).wait_recv()
         build(owner, gland[owner])
-        if ratio == 2:
-            for h in range(2):
-                add(group, h, first=n == 0, last=n == outer_e - 1)
-    if ratio != 2:
+        if early:
+            add(group, 0, first=n == 0, last=n == outer_e - 1)
+            if n < len(late):
+                forward_x(*late[n])
+    if early:
+        add(groups[-1], 1, last=True)
+    else:
+        arrived(1)
         for d in range(n_shot):
             for h in range(2):
                 add(d, h, first=d == 0, last=d == n_shot - 1)
@@ -298,9 +312,9 @@
             pltpu.VMEM((shots * rows_e, LANES), f32),
             tiled(taps, rows_e * shots),
             pltpu.VMEM((tiles * rows_e, LANES), f32),
-            tiled(rows_d * rcv, samples),
-            tiled(samples, rcv * rows_d),
-            tiled(rows, width),
+            tiled(rows_d * rcv, samples // chunks),
+            tiled(samples // chunks, rcv * rows_d),
+            tiled(rows // chunks, width),
             pltpu.VMEM((rows, width), bf16),
             pltpu.VMEM((tiles * rows_e, LANES), bf16),
             pltpu.VMEM((n_shot, rows, width), bf16),

time: 21 us -> 22.7 us (1.081)
  Pallas kernels: 20.7 us -> 22.6 us
    pallas_call x1, Pallas kernels: 18.4 us -> 20.2 us  [shards(): pl.pallas_call(functools.partial(predict, n_shot, n_rcv, chunks), out_sha...]
where the time goes in v4:
time: 22.7 us; the launch traced here: 22.6 us
  Pallas kernels  22.6 us (100%)
    pallas_call x1, Pallas kernels, shards(): pl.pallas_call(functools.partial(predict, n_shot, n_rcv, chunks), out_sha...  20.2 us
    pallas_call x1, Pallas kernels, shards(): pl.pallas_call(arrange, out_shape=jax.ShapeDtypeStruct((shots, rcv, sampl...  2.38 us

profile of v4, /device:TPU:0, one launch (start us, length us, event | category | flops | bytes accessed | tf_op | source)
XLA Modules:
  0.0 22.6 jit_solution(9624717500907153546)
XLA Ops:
  0.0 20.2 %shard_map.28.y_ref = bf16[512,256]{1,0:T(8,128)(2,1)} custom-call(bf16[32,16,64]{2,1,0:T(8,128)(2,1)} %response_hbm.1, bf16[32,8,512]{2,1,0:T(8,128)(2,1)} %traces_hbm.1), custom_call_target="tpu_custom_call" | custom-call | tf_op jit(solution)/shard_map/pallas_call | solution.py:304
  20.2 2.4 %shard_map.29 = bf16[32,8,512]{2,1,0:T(8,128)(2,1)} custom-call(bf16[512,256]{1,0:T(8,128)(2,1)} %shard_map.28.y_ref), custom_call_target="tpu_custom_call" | custom-call | tf_op jit(solution)/shard_map/pallas_call | solution.py:336

commit v5 on v3

--- a/solution.py
+++ b/solution.py
@@ -156,10 +156,15 @@
         go(gcopy(g_ref, me_e, gsend.at[i], (me_d, at_e(i))))
     go(gcopy(g_ref, me_e, gsend.at[0], (me_d, mate_e)))
     fetch_t.wait()
-    x_ref[...] = turn_traces(traces_ref[...], phases, a_ref, z_ref, w_ref)
-    for c in range(chunks):
-        for i in range(1, outer_d):
-            go(xcopy(x_ref, me_d, c, xsend.at[i, c], (at_d(i), me_e)))
+    span = samples // chunks
+    for c in range(chunks + 1):
+        if c < chunks:
+            x_ref[pl.ds(c * part, part), :] = turn_traces(
+                traces_ref[:, :, pl.ds(c * span, span)], phases, a_ref, z_ref, w_ref
+            )
+        if c > 0:
+            for i in range(1, outer_d):
+                go(xcopy(x_ref, me_d, c - 1, xsend.at[i, c - 1], (at_d(i), me_e)))
     for c in range(chunks):
         go(xcopy(x_ref, me_d, c, xsend.at[0, c], (mate_d, me_e)))
 
@@ -233,13 +238,13 @@
 
     todo = [(i, c) for c in range(chunks) for i in range(1, outer_d)]
     for n in range(max(outer_e - 1, len(todo))):
+        if n < len(todo):
+            forward_x(*todo[n])
         if n < outer_e - 1:
             owner = at_e(-order[n])
             copy = gcopy(gland.at[owner], owner, gfwd.at[n], (me_d, mate_e))
             copy.wait_recv()
             go(copy)
-        if n < len(todo):
-            forward_x(*todo[n])
         if n < outer_e - 1:
             build(owner, gland[owner])
     arrived(mate_d)
@@ -298,9 +303,9 @@
             pltpu.VMEM((shots * rows_e, LANES), f32),
             tiled(taps, rows_e * shots),
             pltpu.VMEM((tiles * rows_e, LANES), f32),
-            tiled(rows_d * rcv, samples),
-            tiled(samples, rcv * rows_d),
-            tiled(rows, width),
+            tiled(rows_d * rcv, samples // chunks),
+            tiled(samples // chunks, rcv * rows_d),
+            tiled(rows // chunks, width),
             pltpu.VMEM((rows, width), bf16),
             pltpu.VMEM((tiles * rows_e, LANES), bf16),
             pltpu.VMEM((n_shot, rows, width), bf16),

time: 21 us -> 20.9 us (level)
  no operation moved by 1% of the time
where the time goes in v5:
time: 20.9 us; the launch traced here: 20.7 us
  Pallas kernels  20.7 us (99%)
    pallas_call x1, Pallas kernels, shards(): pl.pallas_call(functools.partial(predict, n_shot, n_rcv, chunks), out_sha...  18.4 us
    pallas_call x1, Pallas kernels, shards(): pl.pallas_call(arrange, out_shape=jax.ShapeDtypeStruct((shots, rcv, sampl...  2.38 us

profile of v5, /device:TPU:0, one launch (start us, length us, event | category | flops | bytes accessed | tf_op | source)
XLA Modules:
  0.0 20.7 jit_solution(15775026071457982487)
XLA Ops:
  0.0 18.4 %shard_map.28.y_ref = bf16[512,256]{1,0:T(8,128)(2,1)} custom-call(bf16[32,16,64]{2,1,0:T(8,128)(2,1)} %response_hbm.1, bf16[32,8,512]{2,1,0:T(8,128)(2,1)} %traces_hbm.1), custom_call_target="tpu_custom_call" | custom-call | tf_op jit(solution)/shard_map/pallas_call | solution.py:295
  18.4 2.4 %shard_map.29 = bf16[32,8,512]{2,1,0:T(8,128)(2,1)} custom-call(bf16[512,256]{1,0:T(8,128)(2,1)} %shard_map.28.y_ref), custom_call_target="tpu_custom_call" | custom-call | tf_op jit(solution)/shard_map/pallas_call | solution.py:327

commit v6 on v5

--- a/solution.py
+++ b/solution.py
@@ -247,6 +247,12 @@
             go(copy)
         if n < outer_e - 1:
             build(owner, gland[owner])
+    def meet(group):
+        owner = group * 2 + 1 - in_e
+        gcopy(g_ref, owner, gsend.at[0], (me_d, mate_e)).wait_recv()
+        build(owner, gland[owner])
+
+    meet(out_e)
     arrived(mate_d)
     bring(mate_d)
     for i in range(1, outer_d):
@@ -258,9 +264,8 @@
 
     for n, i in enumerate([0] + order):
         group = lax.rem(out_e - i + outer_e, outer_e)
-        owner = group * 2 + 1 - in_e
-        gcopy(g_ref, owner, gsend.at[0], (me_d, mate_e)).wait_recv()
-        build(owner, gland[owner])
+        if n > 0:
+            meet(group)
         if ratio == 2:
             for h in range(2):
                 add(group, h, first=n == 0, last=n == outer_e - 1)

time: 20.9 us -> 20.9 us (level)
  no operation moved by 1% of the time
where the time goes in v6:
time: 20.9 us; the launch traced here: 20.7 us
  Pallas kernels  20.7 us (99%)
    pallas_call x1, Pallas kernels, shards(): pl.pallas_call(functools.partial(predict, n_shot, n_rcv, chunks), out_sha...  18.4 us
    pallas_call x1, Pallas kernels, shards(): pl.pallas_call(arrange, out_shape=jax.ShapeDtypeStruct((shots, rcv, sampl...  2.38 us

profile of v6, /device:TPU:0, one launch (start us, length us, event | category | flops | bytes accessed | tf_op | source)
XLA Modules:
  0.0 20.7 jit_solution(4371774565217377020)
XLA Ops:
  0.0 18.4 %shard_map.28.y_ref = bf16[512,256]{1,0:T(8,128)(2,1)} custom-call(bf16[32,16,64]{2,1,0:T(8,128)(2,1)} %response_hbm.1, bf16[32,8,512]{2,1,0:T(8,128)(2,1)} %traces_hbm.1), custom_call_target="tpu_custom_call" | custom-call | tf_op jit(solution)/shard_map/pallas_call | solution.py:300
  18.4 2.4 %shard_map.29 = bf16[32,8,512]{2,1,0:T(8,128)(2,1)} custom-call(bf16[512,256]{1,0:T(8,128)(2,1)} %shard_map.28.y_ref), custom_call_target="tpu_custom_call" | custom-call | tf_op jit(solution)/shard_map/pallas_call | solution.py:332
